TPU v7x, 32 devices: a whole 2x2x4 slice. The times are simulated.
32 devices in a mesh: dp: 8 (over z, x), seq: 4 (over y, core).
Axes of the slice: x: 2, y: 2, z: 4, core: 2. Of those that a mesh axis runs over, the one named last changes fastest.
Arguments:
- queries: bfloat16 [8, 512, 2048], P('dp', 'seq'), may hold values from -72 to 72
- hit_keys: bfloat16 [8, 512, 2048], P('dp', 'seq'), may hold values from -12 to 12
- hit_values: bfloat16 [8, 512, 2048], P('dp', 'seq'), may hold values from -6 to 6
- hit_counts: int32 [8], P('dp'), may hold values from 128 to 512, as said below
- master_weight: float32 [8, 256, 2048], P('dp', None, 'seq'), may hold values from -0.5 to 0.5
- first_moment: float32 [8, 256, 2048], P('dp', None, 'seq'), may hold values from -4 to 4
- second_moment: float32 [8, 256, 2048], P('dp', None, 'seq'), may hold values from 0.1 to 4
- gradient: float32 [8, 256, 2048], P('dp', None, 'seq'), may hold values from -6 to 6
- owner_bucket: int32 [8], replicated, may hold values from 0 to 7, each once
Outputs:
- projected: bfloat16 [8, 512, 2048], P('dp', 'seq')
- new_master: float32 [8, 256, 2048], P('dp', None, 'seq')
- new_first: float32 [8, 256, 2048], P('dp', None, 'seq')
- new_second: float32 [8, 256, 2048], P('dp', None, 'seq')
Inputs may be any that keep to these rules, and one draw needn't show every extreme that they name: The valid hits of event e are its first hit_counts[e] slots; some event is full. `owner_bucket`: each bucket is held by exactly one owner.
All inputs are finite; a program needn't handle non-finite values.
Results may differ from a plain program's by a relative error of at most 0.0063.
Values may be sent and summed in bfloat16 or wider, within the bound.
No kernel may reach another device: no remote copies, remote signals or barrier semaphores. Data moves between devices by JAX's collectives and lax.ppermute only.
A program may use at most 64 MiB of HBM per device.

v0:
```python
import jax
import jax.numpy as jnp
from jax import lax
from jax.sharding import PartitionSpec as P

HEAD_DIM = 128
beta_one = 0.9
beta_two = 0.999
learn_rate = 0.003
weight_decay = 0.1
epsilon = 1e-08
step_count = 10.0
block_rows = 512


def adam_update(master_weight, first_moment, second_moment, gradient):
    new_first = beta_one * first_moment + (1.0 - beta_one) * gradient
    new_second = beta_two * second_moment + (1.0 - beta_two) * gradient * gradient
    first_hat = new_first / (1.0 - beta_one**step_count)
    second_hat = new_second / (1.0 - beta_two**step_count)
    new_master = master_weight - learn_rate * (
        first_hat / (jnp.sqrt(second_hat) + epsilon) + weight_decay * master_weight
    )
    return (new_master, new_first, new_second)


def attend_head(head_query, head_keys, head_values, count):
    length = head_query.shape[0]
    block = min(block_rows, length)
    scale = head_query.shape[1] ** (-0.5)
    valid = lax.broadcasted_iota(jnp.int32, (1, length), 1) < count

    def one_block(rows):
        scores = (
            lax.dot_general(
                rows, head_keys, (((1,), (1,)), ((), ())), preferred_element_type=jnp.float32
            )
            * scale
        )
        scores = jnp.where(valid, scores, -jnp.inf)
        top = jnp.max(scores, axis=1, keepdims=True)
        expo = jnp.exp(scores - top)
        weights = (expo / jnp.sum(expo, axis=1, keepdims=True)).astype(jnp.bfloat16)
        return jnp.dot(weights, head_values, preferred_element_type=jnp.float32).astype(
            jnp.bfloat16
        )

    blocks = head_query.reshape(length // block, block, head_query.shape[1])
    return lax.map(one_block, blocks).reshape(length, head_query.shape[1])


def body(
    queries,
    hit_keys,
    hit_values,
    hit_counts,
    master_weight,
    first_moment,
    second_moment,
    gradient,
    owner_bucket,
):
    new_master, new_first, new_second = adam_update(
        master_weight, first_moment, second_moment, gradient
    )
    weight_half = new_master.astype(jnp.bfloat16)
    groups = lax.axis_size("seq")
    owners = lax.axis_size("dp")
    tok_rows = queries.shape[1]
    width = queries.shape[2]
    per_group = width // groups
    heads_here = per_group // HEAD_DIM
    count = hit_counts[0]
    matches = owner_bucket[:, None] == jnp.arange(owners, dtype=jnp.int32)[None, :]
    inverse = jnp.sum(jnp.where(matches, jnp.arange(owners, dtype=jnp.int32)[:, None], 0), axis=0)

    def split_heads(array):
        return array.reshape(1, tok_rows, groups, heads_here, HEAD_DIM)

    query_part = lax.all_to_all(
        split_heads(queries), "seq", split_axis=2, concat_axis=1, tiled=True
    )
    keys_part = lax.all_to_all(
        split_heads(hit_keys), "seq", split_axis=2, concat_axis=1, tiled=True
    )
    values_part = lax.all_to_all(
        split_heads(hit_values), "seq", split_axis=2, concat_axis=1, tiled=True
    )
    n_heads = query_part.shape[3]

    def one_head(index):
        head_query = lax.dynamic_index_in_dim(query_part, index, 3, keepdims=False)[0, :, 0, :]
        head_keys = lax.dynamic_index_in_dim(keys_part, index, 3, keepdims=False)[0, :, 0, :]
        head_values = lax.dynamic_index_in_dim(values_part, index, 3, keepdims=False)[0, :, 0, :]
        return attend_head(head_query, head_keys, head_values, count)

    outputs = lax.map(one_head, jnp.arange(n_heads, dtype=jnp.int32))
    attended = jnp.moveaxis(outputs, 0, 1)[None, :, None, :, :]
    returned = lax.all_to_all(attended, "seq", split_axis=1, concat_axis=2, tiled=True)
    rows_in = returned.reshape(tok_rows, width)
    owned = lax.all_gather(weight_half, "dp", axis=0, tiled=True)
    full = lax.all_gather(owned, "seq", axis=2, tiled=True)
    projection = jnp.take(full, inverse, axis=0).reshape(width, width)
    total = jnp.dot(rows_in, projection, preferred_element_type=jnp.float32)
    projected = total.astype(jnp.bfloat16)[None]
    return (projected, new_master, new_first, new_second)


def solution(mesh):
    return jax.shard_map(
        body,
        mesh=mesh,
        in_specs=(
            P("dp", "seq", None),
            P("dp", "seq", None),
            P("dp", "seq", None),
            P("dp"),
            P("dp", None, "seq"),
            P("dp", None, "seq"),
            P("dp", None, "seq"),
            P("dp", None, "seq"),
            P(),
        ),
        out_specs=(
            P("dp", "seq", None),
            P("dp", None, "seq"),
            P("dp", None, "seq"),
            P("dp", None, "seq"),
        ),
        check_vma=False,
    )
```

profile of v0, /device:TPU:0, one launch (start us, length us, event | category | flops | bytes accessed | tf_op | source)
XLA Modules:
  0.0 175.6 jit_solution(9775890406966182870)
XLA Ops:
  7.2 3.1 %fusion.15 = (bf16[1,256,512]{2,1,0:T(8,128)(2,1)}, f32[1,256,512]{2,1,0:T(8,128)}, f32[1,256,512]{2,1,0:T(8,128)}, f32[1,256,512]{2,1,0:T(8,128)}) fusion(f32[1,256,512]{2,1,0:T(8,128)} %param.15, f32[1,256,512]{2,1,0:T(8,128)} %param.18, f32[1,256,512]{2,1,0:T(8,128)} %param.16, f32[1,256,512]{2,1,0:T(8,128)} %param.17), kind=kLoop, calls=%fused_computation.33 | loop fusion | flops 2097152 | bytes 3932160 | tf_op jit(solution)/shard_map/convert_element_type | solution.py:66
  10.4 52.3 %all-gather.3.cloned.1.call-done = bf16[8,256,512]{2,1,0:T(8,128)(2,1)} async-done(((bf16[1,256,512]{2,1,0:T(8,128)(2,1)}), bf16[8,256,512]{2,1,0:T(8,128)(2,1)}) %all-gather.3.cloned.1.call-update) | async-done | bytes 2097168 | tf_op jit(solution)/shard_map/all_gather | solution.py:101
  62.8 1.3 copy.41
  64.1 1.0 copy.42
  65.1 3.5 %all-to-all-start.1 = ((bf16[1,128,4,4,128]{4,1,3,0,2:T(8,128)(2,1)}), bf16[1,128,4,4,128]{4,1,3,0,2:T(8,128)(2,1)S(1)}, u32[]{:S(2)}, u32[]{:S(2)}) async-start(bf16[1,128,4,4,128]{4,1,3,0,2:T(8,128)(2,1)} %copy.42), calls=%async_computation.1 | async-start | bytes 1048576 | tf_op jit(solution)/shard_map/all_to_all | solution.py:83
  68.9 1.0 copy.45
  69.9 10.8 %all-to-all-done.1 = bf16[1,128,4,4,128]{4,1,3,0,2:T(8,128)(2,1)S(1)} async-done(((bf16[1,128,4,4,128]{4,1,3,0,2:T(8,128)(2,1)}), bf16[1,128,4,4,128]{4,1,3,0,2:T(8,128)(2,1)S(1)}, u32[]{:S(2)}, u32[]{:S(2)}) %all-to-all-start.1) | async-done | bytes 524320 | tf_op jit(solution)/shard_map/all_to_all | solution.py:83
  80.7 3.5 %all-to-all-start.2 = ((bf16[1,128,4,4,128]{4,1,3,0,2:T(8,128)(2,1)}), bf16[1,128,4,4,128]{4,1,3,0,2:T(8,128)(2,1)S(1)}, u32[]{:S(2)}, u32[]{:S(2)}) async-start(bf16[1,128,4,4,128]{4,1,3,0,2:T(8,128)(2,1)} %copy.45), calls=%async_computation.2 | async-start | bytes 1048576 | tf_op jit(solution)/shard_map/all_to_all | solution.py:86
  84.5 1.0 copy.39
  85.5 13.4 %all-to-all-done.2 = bf16[1,128,4,4,128]{4,1,3,0,2:T(8,128)(2,1)S(1)} async-done(((bf16[1,128,4,4,128]{4,1,3,0,2:T(8,128)(2,1)}), bf16[1,128,4,4,128]{4,1,3,0,2:T(8,128)(2,1)S(1)}, u32[]{:S(2)}, u32[]{:S(2)}) %all-to-all-start.2) | async-done | bytes 524320 | tf_op jit(solution)/shard_map/all_to_all | solution.py:86
  99.0 3.5 %all-to-all-start = ((bf16[1,128,4,4,128]{4,1,3,0,2:T(8,128)(2,1)}), bf16[1,128,4,4,128]{4,1,3,0,2:T(8,128)(2,1)S(1)}, u32[]{:S(2)}, u32[]{:S(2)}) async-start(bf16[1,128,4,4,128]{4,1,3,0,2:T(8,128)(2,1)} %copy.39), calls=%async_computation | async-start | bytes 1048576 | tf_op jit(solution)/shard_map/all_to_all | solution.py:80
  102.6 14.5 %all-to-all-done = bf16[1,128,4,4,128]{4,1,3,0,2:T(8,128)(2,1)S(1)} async-done(((bf16[1,128,4,4,128]{4,1,3,0,2:T(8,128)(2,1)}), bf16[1,128,4,4,128]{4,1,3,0,2:T(8,128)(2,1)S(1)}, u32[]{:S(2)}, u32[]{:S(2)}) %all-to-all-start) | async-done | bytes 524320 | tf_op jit(solution)/shard_map/all_to_all | solution.py:80
  117.2 16.6 %while.10 = (s32[]{:T(128)}, bf16[4,512,128]{2,1,0:T(8,128)(2,1)S(1)}, s32[]{:T(128)}, s32[4]{0:T(128)S(1)}, bf16[1,512,1,4,128]{4,1,3,2,0:T(8,128)(2,1)S(1)}, /...) while((s32[]{:T(128)}, ...), condition=%wide.region_3.4_spmd, body=%wide.region_0.3_spmd.sunk | while | flops 136379904 | bytes 3682463 | solution.py:97
  117.3 0.6 dynamic_slice.40
  119.8 0.7 iota_compare_fusion.3
  121.0 0.4 fusion.27
  121.4 0.6 dynamic_slice.40
  123.9 0.7 iota_compare_fusion.3
  125.1 0.4 fusion.27
  125.6 0.6 dynamic_slice.40
  128.1 0.7 iota_compare_fusion.3
  128.8 0.3 fusion.25
  129.3 0.4 fusion.27
  129.7 0.6 dynamic_slice.40
  132.3 0.7 iota_compare_fusion.3
  133.4 0.4 fusion.27
  133.9 1.2 copy.51
  135.1 3.5 %all-to-all-start.3 = ((bf16[1,512,1,4,128]{4,3,2,0,1:T(4,128)(2,1)}), bf16[1,512,1,4,128]{4,3,2,0,1:T(4,128)(2,1)S(1)}, u32[]{:S(2)}, u32[]{:S(2)}) async-start(bf16[1,512,1,4,128]{4,3,2,0,1:T(4,128)(2,1)} %bitcast.54), calls=%async_computation.3 | async-start | bytes 1048576 | tf_op jit(solution)/shard_map/all_to_all | solution.py:99
  138.6 8.8 %all-to-all-done.3 = bf16[1,512,1,4,128]{4,3,2,0,1:T(4,128)(2,1)S(1)} async-done(((bf16[1,512,1,4,128]{4,3,2,0,1:T(4,128)(2,1)}), bf16[1,512,1,4,128]{4,3,2,0,1:T(4,128)(2,1)S(1)}, u32[]{:S(2)}, u32[]{:S(2)}) %all-to-all-start.3) | async-done | bytes 524320 | tf_op jit(solution)/shard_map/all_to_all | solution.py:99
  147.8 8.1 %gather_fusion = bf16[8,256,2048]{2,1,0:T(8,128)(2,1)} fusion(bf16[8,256,2048]{2,1,0:T(8,128)(2,1)} %all-gather.5.cloned.1.call-done, s32[1024]{0:T(1024)S(1)} %pad_clamp_fusion), kind=kCustom, calls=%fused_computation | custom fusion | bytes 16777248 | tf_op jit(solution)/shard_map/jit(_take)/gather | solution.py:103
  155.8 7.5 %broadcast_select_fusion = bf16[8,256,2048]{2,1,0:T(8,128)(2,1)} fusion(bf16[8,256,2048]{2,1,0:T(8,128)(2,1)} %gather_fusion, pred[8]{0:T(512)(128)(4,1)S(1)} %compare_and_fusion), kind=kLoop, calls=%fused_computation.18 | loop fusion | flops 4194304 | bytes 16777224 | tf_op jit(solution)/shard_map/jit(_take)/select_n | solution.py:103
  163.3 5.5 %fusion.12 = bf16[1,128,2048]{2,1,0:T(8,128)(2,1)} fusion(bf16[128,2048]{0,1:T(8,128)(2,1)S(1)} %bitcast.66, bf16[2048,2048]{1,0:T(8,128)(2,1)} %bitcast.65), kind=kOutput, calls=%fused_computation.20 | convolution fusion | flops 1074003968 | bytes 9437184 | tf_op jit(solution)/shard_map/dot_general | solution.py:104
  (31 shorter events, 3.0 us)
Async XLA Ops:
  7.2 61.4 %copy-start = (bf16[1,128,2048]{2,1,0:T(8,128)(2,1)S(1)}, bf16[1,128,2048]{2,1,0:T(8,128)(2,1)}, u32[]{:S(2)}) copy-start(bf16[1,128,2048]{2,1,0:T(8,128)(2,1)} %param.13) | copy-start | bytes 1572868
  7.2 77.0 %copy-start.1 = (bf16[1,128,2048]{2,1,0:T(8,128)(2,1)S(1)}, bf16[1,128,2048]{2,1,0:T(8,128)(2,1)}, u32[]{:S(2)}) copy-start(bf16[1,128,2048]{2,1,0:T(8,128)(2,1)} %param.11) | copy-start | bytes 1572868
  7.2 95.3 %copy-start.2 = (s32[8]{0:T(128)S(1)}, s32[8]{0:T(128)}, u32[]{:S(2)}) copy-start(s32[8]{0:T(128)} %param.19) | copy-start | bytes 100
  7.2 55.6 %all-gather.3.cloned.1.call-start = ((), (), s32[]{:S(2)}) async-start(), calls=%async_computation.4 | async-start | bytes 2359296 | tf_op jit(solution)/shard_map/all_gather | solution.py:101
  10.4 137.4 %all-gather.5.cloned.1.call-start = ((), (), s32[]{:S(2)}) async-start(), calls=%async_computation.5 | async-start | bytes 10485760 | tf_op jit(solution)/shard_map/all_gather | solution.py:102
  65.1 15.6 %all-to-all-start.1 = ((bf16[1,128,4,4,128]{4,1,3,0,2:T(8,128)(2,1)}), bf16[1,128,4,4,128]{4,1,3,0,2:T(8,128)(2,1)S(1)}, u32[]{:S(2)}, u32[]{:S(2)}) async-start(bf16[1,128,4,4,128]{4,1,3,0,2:T(8,128)(2,1)} %copy.42), calls=%async_computation.1 | async-start | bytes 1048576 | tf_op jit(solution)/shard_map/all_to_all | solution.py:83
  80.7 18.2 %all-to-all-start.2 = ((bf16[1,128,4,4,128]{4,1,3,0,2:T(8,128)(2,1)}), bf16[1,128,4,4,128]{4,1,3,0,2:T(8,128)(2,1)S(1)}, u32[]{:S(2)}, u32[]{:S(2)}) async-start(bf16[1,128,4,4,128]{4,1,3,0,2:T(8,128)(2,1)} %copy.45), calls=%async_computation.2 | async-start | bytes 1048576 | tf_op jit(solution)/shard_map/all_to_all | solution.py:86
  99.0 18.2 %all-to-all-start = ((bf16[1,128,4,4,128]{4,1,3,0,2:T(8,128)(2,1)}), bf16[1,128,4,4,128]{4,1,3,0,2:T(8,128)(2,1)S(1)}, u32[]{:S(2)}, u32[]{:S(2)}) async-start(bf16[1,128,4,4,128]{4,1,3,0,2:T(8,128)(2,1)} %copy.39), calls=%async_computation | async-start | bytes 1048576 | tf_op jit(solution)/shard_map/all_to_all | solution.py:80
  135.1 12.3 %all-to-all-start.3 = ((bf16[1,512,1,4,128]{4,3,2,0,1:T(4,128)(2,1)}), bf16[1,512,1,4,128]{4,3,2,0,1:T(4,128)(2,1)S(1)}, u32[]{:S(2)}, u32[]{:S(2)}) async-start(bf16[1,512,1,4,128]{4,3,2,0,1:T(4,128)(2,1)} %bitcast.54), calls=%async_computation.3 | async-start | bytes 1048576 | tf_op jit(solution)/shard_map/all_to_all | solution.py:99
Sparse Core Ops, SparseCore 0:
  10.7 51.9 all-gather.2
  64.3 71.0 all-gather.4
where the time goes:
time: 176 us
  waiting for transfers between devices  100 us (57%)
  local copies, waits for them, and re-layouts  17 us (10%)
  between operations  14.2 us (8%)
  other arithmetic  14.1 us (8%)
  starting transfers between devices  14 us (8%)
  matrix products  8.47 us (5%)
  loops' own time  7.88 us (4%)
    all_gather x1, waiting for transfers between devices, body(): owned = lax.all_gather(weight_half, 'dp', axis=0, tiled=True)  52.3 us
    all_to_all x1, waiting for transfers between devices, body(): lax.all_to_all(split_heads(queries), 'seq', split_axis=2, concat_axis=1,...  14.5 us
    all_to_all x1, waiting for transfers between devices, body(): lax.all_to_all(split_heads(hit_values), 'seq', split_axis=2, concat_axis=...  13.4 us
    all_to_all x1, waiting for transfers between devices, body(): lax.all_to_all(split_heads(hit_keys), 'seq', split_axis=2, concat_axis=1,...  10.8 us
    all_to_all x1, waiting for transfers between devices, body(): lax.all_to_all(attended, 'seq', split_axis=1, concat_axis=2, tiled=True)  8.77 us
    gather x1, local copies, waits for them, and re-layouts, body(): projection = jnp.take(full, inverse, axis=0).reshape(width, width)  8.08 us
    another operation x1, loops' own time, body(): outputs = lax.map(one_head, jnp.arange(n_heads, dtype=jnp.int32))  7.88 us
    select_n x2, other arithmetic, body(): projection = jnp.take(full, inverse, axis=0).reshape(width, width)  7.49 us
  transfers between devices with their start and end apart: 6, of which 5 were waited for; matrix products, arithmetic and copies ran while one was open for 9% of the time, Pallas kernels for 0%

commit v1 on v0

--- a/solution.py
+++ b/solution.py
@@ -1,3 +1,4 @@
+import functools
 import jax
 import jax.numpy as jnp
 from jax import lax
@@ -11,6 +12,39 @@
 epsilon = 1e-08
 step_count = 10.0
 block_rows = 512
+
+
+def _touch_view(message, out_dim, page):
+    t_next = message.shape
+    fresh = message.reshape(
+        *t_next[:out_dim], page, t_next[out_dim] // page, *t_next[out_dim + 1 :]
+    )
+    return jnp.moveaxis(fresh, out_dim, 0)
+
+
+def ratios_feed(mine, along_dim):
+    mine = jnp.moveaxis(mine, 0, along_dim)
+    moved = mine.shape
+    return mine.reshape(
+        *moved[:along_dim], moved[along_dim] * moved[along_dim + 1], *moved[along_dim + 2 :]
+    )
+
+
+def spans_fill(my_data, which_axis, v0, patch):
+    found_now = jax.lax.axis_size(which_axis)
+    passed = jax.lax.axis_index(which_axis)
+    arr_now, res = (found_now, passed)
+    current_arr = _touch_view(my_data, v0, arr_now)
+    n_now = current_arr
+    for j in range(1, arr_now):
+        z1, p_next = ((res + j) % arr_now, (res - j) % arr_now)
+        new = lax.dynamic_index_in_dim(current_arr, z1, 0)
+        even = jax.lax.ppermute(new, which_axis, [(b, (b + j) % arr_now) for b in range(arr_now)])
+        n_now = lax.dynamic_update_slice_in_dim(n_now, even, p_next, axis=0)
+    return ratios_feed(n_now, patch)
+
+
+stocks_bind = functools.partial(spans_fill, which_axis="seq", v0=2, patch=1)
 
 
 def adam_update(master_weight, first_moment, second_moment, gradient):
@@ -77,9 +111,7 @@
     def split_heads(array):
         return array.reshape(1, tok_rows, groups, heads_here, HEAD_DIM)
 
-    query_part = lax.all_to_all(
-        split_heads(queries), "seq", split_axis=2, concat_axis=1, tiled=True
-    )
+    query_part = stocks_bind(split_heads(queries))
     keys_part = lax.all_to_all(
         split_heads(hit_keys), "seq", split_axis=2, concat_axis=1, tiled=True
     )

time: 176 us -> 169 us (0.960)
  waiting for transfers between devices: 100 us -> 94.6 us
    all_to_all x1 -> x0, waiting for transfers between devices: 14.5 us -> none  [body(): lax.all_to_all(split_heads(queries), 'seq', split_axis=2, concat_axis=1,...]
    all_to_all x1, waiting for transfers between devices: 8.77 us -> 14.7 us  [body(): lax.all_to_all(attended, 'seq', split_axis=1, concat_axis=2, tiled=True)]
    ppermute x0 -> x3, waiting for transfers between devices: none -> 4.84 us  [spans_fill(): jax.lax.ppermute(new, which_axis, [(b, (b + j) % arr_now) for b in range(...]
    all_to_all x1, waiting for transfers between devices: 10.8 us -> 7.08 us  [body(): lax.all_to_all(split_heads(hit_keys), 'seq', split_axis=2, concat_axis=1,...]
    ppermute x0 -> x3, starting transfers between devices: none -> 3.57 us  [spans_fill(): jax.lax.ppermute(new, which_axis, [(b, (b + j) % arr_now) for b in range(...]
    all_to_all x1 -> x0, starting transfers between devices: 3.47 us -> none  [body(): lax.all_to_all(split_heads(queries), 'seq', split_axis=2, concat_axis=1,...]
    all_gather x1, waiting for transfers between devices: 0.02 us -> 2.36 us  [body(): full = lax.all_gather(owned, 'seq', axis=2, tiled=True)]
  transfers between devices with their start and end apart: 6 -> 8, of which waited for: 5 -> 7; matrix products, arithmetic and copies ran while one was open for 9% -> 9% of each run, Pallas kernels for 0% -> 0%
where the time goes in v1:
time: 169 us
  waiting for transfers between devices  94.6 us (56%)
  local copies, waits for them, and re-layouts  16.4 us (10%)
  between operations  14.3 us (8%)
  starting transfers between devices  14.1 us (8%)
  other arithmetic  14.1 us (8%)
  matrix products  8.46 us (5%)
  loops' own time  6.83 us (4%)
    all_gather x1, waiting for transfers between devices, body(): owned = lax.all_gather(weight_half, 'dp', axis=0, tiled=True)  52.3 us
    all_to_all x1, waiting for transfers between devices, body(): lax.all_to_all(attended, 'seq', split_axis=1, concat_axis=2, tiled=True)  14.7 us
    all_to_all x1, waiting for transfers between devices, body(): lax.all_to_all(split_heads(hit_values), 'seq', split_axis=2, concat_axis=...  13.3 us
    gather x1, local copies, waits for them, and re-layouts, body(): projection = jnp.take(full, inverse, axis=0).reshape(width, width)  8.06 us
    select_n x2, other arithmetic, body(): projection = jnp.take(full, inverse, axis=0).reshape(width, width)  7.48 us
    all_to_all x1, waiting for transfers between devices, body(): lax.all_to_all(split_heads(hit_keys), 'seq', split_axis=2, concat_axis=1,...  7.08 us
    another operation x1, loops' own time, body(): outputs = lax.map(one_head, jnp.arange(n_heads, dtype=jnp.int32))  6.83 us
    dot_general x1, matrix products, body(): total = jnp.dot(rows_in, projection, preferred_element_type=jnp.float32)  5.46 us
  transfers between devices with their start and end apart: 8, of which 7 were waited for; matrix products, arithmetic and copies ran while one was open for 9% of the time, Pallas kernels for 0%

profile of v1, /device:TPU:0, one launch (start us, length us, event | category | flops | bytes accessed | tf_op | source)
XLA Modules:
  0.0 168.8 jit_solution(5370804993864776043)
XLA Ops:
  7.2 3.1 %fusion.15 = (bf16[1,256,512]{2,1,0:T(8,128)(2,1)}, f32[1,256,512]{2,1,0:T(8,128)}, f32[1,256,512]{2,1,0:T(8,128)}, f32[1,256,512]{2,1,0:T(8,128)}) fusion(f32[1,256,512]{2,1,0:T(8,128)} %param.15, f32[1,256,512]{2,1,0:T(8,128)} %param.18, f32[1,256,512]{2,1,0:T(8,128)} %param.16, f32[1,256,512]{2,1,0:T(8,128)} %param.17), kind=kLoop, calls=%fused_computation.43 | loop fusion | flops 2097152 | bytes 3932160 | tf_op jit(solution)/shard_map/convert_element_type | solution.py:100
  10.4 52.3 %all-gather.3.cloned.1.call-done = bf16[8,256,512]{2,1,0:T(8,128)(2,1)} async-done(((bf16[1,256,512]{2,1,0:T(8,128)(2,1)}), bf16[8,256,512]{2,1,0:T(8,128)(2,1)}) %all-gather.3.cloned.1.call-update) | async-done | bytes 2097168 | tf_op jit(solution)/shard_map/all_gather | solution.py:133
  62.8 1.3 copy.53
  64.1 1.0 copy.54
  65.1 3.5 %all-to-all-start = ((bf16[1,128,4,4,128]{4,1,3,0,2:T(8,128)(2,1)}), bf16[1,128,4,4,128]{4,1,3,0,2:T(8,128)(2,1)S(1)}, u32[]{:S(2)}, u32[]{:S(2)}) async-start(bf16[1,128,4,4,128]{4,1,3,0,2:T(8,128)(2,1)} %copy.54), calls=%async_computation | async-start | bytes 1048576 | tf_op jit(solution)/shard_map/all_to_all | solution.py:115
  69.2 0.5 collective-permute-start
  69.7 1.7 %collective-permute-start.1 = (bf16[1,1,128,1,4,128]{5,2,0,4,3,1:T(8,128)(2,1)S(1)}, bf16[1,1,128,1,4,128]{5,2,0,4,3,1:T(8,128)(2,1)S(1)}, u32[]{:S(2)}, u32[]{:S(2)}) collective-permute-start(bf16[1,1,128,1,4,128]{5,2,0,4,3,1:T(8,128)(2,1)S(1)} %bitcast.82), channel_id=1, source_target_pairs={{0,2},{1,3},{2,0},{3,1},{4,6},{5,7},{6,4},{7,5},{8,10},{9,11},{10,... | collective-permute-start | bytes 393224 | tf_op jit(solution)/shard_map/ppermute | solution.py:42
  71.5 1.4 collective-permute-start.2
  73.1 1.0 copy.57
  74.1 7.1 %all-to-all-done = bf16[1,128,4,4,128]{4,1,3,0,2:T(8,128)(2,1)S(1)} async-done(((bf16[1,128,4,4,128]{4,1,3,0,2:T(8,128)(2,1)}), bf16[1,128,4,4,128]{4,1,3,0,2:T(8,128)(2,1)S(1)}, u32[]{:S(2)}, u32[]{:S(2)}) %all-to-all-start) | async-done | bytes 524320 | tf_op jit(solution)/shard_map/all_to_all | solution.py:115
  81.2 3.5 %all-to-all-start.1 = ((bf16[1,128,4,4,128]{4,1,3,0,2:T(8,128)(2,1)}), bf16[1,128,4,4,128]{4,1,3,0,2:T(8,128)(2,1)S(1)}, u32[]{:S(2)}, u32[]{:S(2)}) async-start(bf16[1,128,4,4,128]{4,1,3,0,2:T(8,128)(2,1)} %copy.57), calls=%async_computation.1 | async-start | bytes 1048576 | tf_op jit(solution)/shard_map/all_to_all | solution.py:118
  85.0 1.8 %collective-permute-done.1 = bf16[1,1,128,1,4,128]{5,2,0,4,3,1:T(8,128)(2,1)S(1)} collective-permute-done((bf16[1,1,128,1,4,128]{5,2,0,4,3,1:T(8,128)(2,1)S(1)}, bf16[1,1,128,1,4,128]{5,2,0,4,3,1:T(8,128)(2,1)S(1)}, u32[]{:S(2)}, u32[]{:S(2)}) %collective-permute-start.1) | collective-permute-done | bytes 131104 | tf_op jit(solution)/shard_map/ppermute | solution.py:42
  86.8 3.0 %collective-permute-done.2 = bf16[1,1,128,1,4,128]{5,2,0,4,3,1:T(8,128)(2,1)S(1)} collective-permute-done((bf16[1,1,128,1,4,128]{5,2,0,4,3,1:T(8,128)(2,1)S(1)}, bf16[1,1,128,1,4,128]{5,2,0,4,3,1:T(8,128)(2,1)S(1)}, u32[]{:S(2)}, u32[]{:S(2)}) %collective-permute-start.2) | collective-permute-done | bytes 131104 | tf_op jit(solution)/shard_map/ppermute | solution.py:42
  89.9 13.3 %all-to-all-done.1 = bf16[1,128,4,4,128]{4,1,3,0,2:T(8,128)(2,1)S(1)} async-done(((bf16[1,128,4,4,128]{4,1,3,0,2:T(8,128)(2,1)}), bf16[1,128,4,4,128]{4,1,3,0,2:T(8,128)(2,1)S(1)}, u32[]{:S(2)}, u32[]{:S(2)}) %all-to-all-start.1) | async-done | bytes 524320 | tf_op jit(solution)/shard_map/all_to_all | solution.py:118
  103.3 15.6 %while.10 = (s32[]{:T(128)}, bf16[4,512,128]{2,1,0:T(8,128)(2,1)S(1)}, s32[]{:T(128)}, s32[4]{0:T(128)S(1)}, bf16[1,512,1,4,128]{4,1,3,2,0:T(8,128)(2,1)S(1)}, /...) while((s32[]{:T(128)}, ...), condition=%wide.region_3.4_spmd, body=%wide.region_0.3_spmd.sunk | while | flops 136379904 | bytes 3682471 | solution.py:129
  103.3 0.6 dynamic_slice.53
  105.5 0.7 iota_compare_fusion.3
  107.2 0.6 dynamic_slice.53
  109.4 0.7 iota_compare_fusion.3
  110.6 0.4 fusion.27
  111.0 0.6 dynamic_slice.53
  113.3 0.7 iota_compare_fusion.3
  114.5 0.4 fusion.27
  114.9 0.6 dynamic_slice.53
  117.2 0.7 iota_compare_fusion.3
  118.8 1.2 copy.67
  120.0 3.5 %all-to-all-start.2 = ((bf16[1,512,1,4,128]{4,3,2,0,1:T(4,128)(2,1)}), bf16[1,512,1,4,128]{4,3,2,0,1:T(4,128)(2,1)S(1)}, u32[]{:S(2)}, u32[]{:S(2)}) async-start(bf16[1,512,1,4,128]{4,3,2,0,1:T(4,128)(2,1)} %bitcast.57), calls=%async_computation.2 | async-start | bytes 1048576 | tf_op jit(solution)/shard_map/all_to_all | solution.py:131
  123.5 14.7 %all-to-all-done.2 = bf16[1,512,1,4,128]{4,3,2,0,1:T(4,128)(2,1)S(1)} async-done(((bf16[1,512,1,4,128]{4,3,2,0,1:T(4,128)(2,1)}), bf16[1,512,1,4,128]{4,3,2,0,1:T(4,128)(2,1)S(1)}, u32[]{:S(2)}, u32[]{:S(2)}) %all-to-all-start.2) | async-done | bytes 524320 | tf_op jit(solution)/shard_map/all_to_all | solution.py:131
  138.6 2.4 %all-gather.5.cloned.1.call-done = bf16[8,256,2048]{2,1,0:T(8,128)(2,1)} async-done(((bf16[8,256,512]{2,1,0:T(8,128)(2,1)}), bf16[8,256,2048]{2,1,0:T(8,128)(2,1)}) %all-gather.5.cloned.1.call-update) | async-done | bytes 8388624 | tf_op jit(solution)/shard_map/all_gather | solution.py:134
  141.0 8.1 %gather_fusion = bf16[8,256,2048]{2,1,0:T(8,128)(2,1)} fusion(bf16[8,256,2048]{2,1,0:T(8,128)(2,1)} %all-gather.5.cloned.1.call-done, s32[1024]{0:T(1024)S(1)} %pad_clamp_fusion), kind=kCustom, calls=%fused_computation | custom fusion | bytes 16777248 | tf_op jit(solution)/shard_map/jit(_take)/gather | solution.py:135
  149.0 7.5 %broadcast_select_fusion = bf16[8,256,2048]{2,1,0:T(8,128)(2,1)} fusion(bf16[8,256,2048]{2,1,0:T(8,128)(2,1)} %gather_fusion, pred[8]{0:T(512)(128)(4,1)S(1)} %compare_and_fusion), kind=kLoop, calls=%fused_computation.18 | loop fusion | flops 4194304 | bytes 16777224 | tf_op jit(solution)/shard_map/jit(_take)/select_n | solution.py:135
  156.5 5.5 %fusion.12 = bf16[1,128,2048]{2,1,0:T(8,128)(2,1)} fusion(bf16[128,2048]{0,1:T(8,128)(2,1)S(1)} %bitcast.73, bf16[2048,2048]{1,0:T(8,128)(2,1)} %bitcast.72), kind=kOutput, calls=%fused_computation.20 | convolution fusion | flops 1074003968 | bytes 9437184 | tf_op jit(solution)/shard_map/dot_general | solution.py:136
  (41 shorter events, 4.6 us)
Async XLA Ops:
  7.2 61.5 %copy-start = (bf16[1,128,2048]{2,1,0:T(8,128)(2,1)S(1)}, bf16[1,128,2048]{2,1,0:T(8,128)(2,1)}, u32[]{:S(2)}) copy-start(bf16[1,128,2048]{2,1,0:T(8,128)(2,1)} %param.11) | copy-start | bytes 1572868
  7.2 65.6 %copy-start.1 = (bf16[1,128,2048]{2,1,0:T(8,128)(2,1)S(1)}, bf16[1,128,2048]{2,1,0:T(8,128)(2,1)}, u32[]{:S(2)}) copy-start(bf16[1,128,2048]{2,1,0:T(8,128)(2,1)} %param.13) | copy-start | bytes 1572868
  7.2 77.5 %copy-start.2 = (s32[8]{0:T(128)S(1)}, s32[8]{0:T(128)}, u32[]{:S(2)}) copy-start(s32[8]{0:T(128)} %param.19) | copy-start | bytes 100
  7.2 55.6 %all-gather.3.cloned.1.call-start = ((), (), s32[]{:S(2)}) async-start(), calls=%async_computation.3 | async-start | bytes 2359296 | tf_op jit(solution)/shard_map/all_gather | solution.py:133
  10.4 130.6 %all-gather.5.cloned.1.call-start = ((), (), s32[]{:S(2)}) async-start(), calls=%async_computation.4 | async-start | bytes 10485760 | tf_op jit(solution)/shard_map/all_gather | solution.py:134
  65.1 16.1 %all-to-all-start = ((bf16[1,128,4,4,128]{4,1,3,0,2:T(8,128)(2,1)}), bf16[1,128,4,4,128]{4,1,3,0,2:T(8,128)(2,1)S(1)}, u32[]{:S(2)}, u32[]{:S(2)}) async-start(bf16[1,128,4,4,128]{4,1,3,0,2:T(8,128)(2,1)} %copy.54), calls=%async_computation | async-start | bytes 1048576 | tf_op jit(solution)/shard_map/all_to_all | solution.py:115
  69.2 15.7 %collective-permute-start = (bf16[1,1,128,1,4,128]{5,2,0,4,3,1:T(8,128)(2,1)S(1)}, bf16[1,1,128,1,4,128]{5,2,0,4,3,1:T(8,128)(2,1)S(1)}, u32[]{:S(2)}, u32[]{:S(2)}) collective-permute-start(bf16[1,1,128,1,4,128]{5,2,0,4,3,1:T(8,128)(2,1)S(1)} %bitcast.83), channel_id=1, source_target_pairs={{0,1},{1,2},{2,3},{3,0},{4,5},{5,6},{6,7},{7,4},{8,9},{9,10},{10,1... | collective-permute-start | bytes 393224 | tf_op jit(solution)/shard_map/ppermute | solution.py:42
  69.7 17.1 %collective-permute-start.1 = (bf16[1,1,128,1,4,128]{5,2,0,4,3,1:T(8,128)(2,1)S(1)}, bf16[1,1,128,1,4,128]{5,2,0,4,3,1:T(8,128)(2,1)S(1)}, u32[]{:S(2)}, u32[]{:S(2)}) collective-permute-start(bf16[1,1,128,1,4,128]{5,2,0,4,3,1:T(8,128)(2,1)S(1)} %bitcast.82), channel_id=1, source_target_pairs={{0,2},{1,3},{2,0},{3,1},{4,6},{5,7},{6,4},{7,5},{8,10},{9,11},{10,... | collective-permute-start | bytes 393224 | tf_op jit(solution)/shard_map/ppermute | solution.py:42
  71.5 18.4 %collective-permute-start.2 = (bf16[1,1,128,1,4,128]{5,2,0,4,3,1:T(8,128)(2,1)S(1)}, bf16[1,1,128,1,4,128]{5,2,0,4,3,1:T(8,128)(2,1)S(1)}, u32[]{:S(2)}, u32[]{:S(2)}) collective-permute-start(bf16[1,1,128,1,4,128]{5,2,0,4,3,1:T(8,128)(2,1)S(1)} %bitcast.81), channel_id=1, source_target_pairs={{0,3},{1,0},{2,1},{3,2},{4,7},{5,4},{6,5},{7,6},{8,11},{9,8},{10,9... | collective-permute-start | bytes 393224 | tf_op jit(solution)/shard_map/ppermute | solution.py:42
  81.2 22.0 %all-to-all-start.1 = ((bf16[1,128,4,4,128]{4,1,3,0,2:T(8,128)(2,1)}), bf16[1,128,4,4,128]{4,1,3,0,2:T(8,128)(2,1)S(1)}, u32[]{:S(2)}, u32[]{:S(2)}) async-start(bf16[1,128,4,4,128]{4,1,3,0,2:T(8,128)(2,1)} %copy.57), calls=%async_computation.1 | async-start | bytes 1048576 | tf_op jit(solution)/shard_map/all_to_all | solution.py:118
  120.0 18.2 %all-to-all-start.2 = ((bf16[1,512,1,4,128]{4,3,2,0,1:T(4,128)(2,1)}), bf16[1,512,1,4,128]{4,3,2,0,1:T(4,128)(2,1)S(1)}, u32[]{:S(2)}, u32[]{:S(2)}) async-start(bf16[1,512,1,4,128]{4,3,2,0,1:T(4,128)(2,1)} %bitcast.57), calls=%async_computation.2 | async-start | bytes 1048576 | tf_op jit(solution)/shard_map/all_to_all | solution.py:131
Sparse Core Ops, SparseCore 0:
  10.7 51.9 all-gather.2
  64.3 76.6 all-gather.4
